TPU v7x, 256 devices: a whole 4x4x8 slice. The times are simulated.
256 devices in a mesh: fsdp: 16 (over y, z_lo, core), uly: 4 (over x), blk: 4 (over z_hi).
Axes of the slice: x: 4, y: 4, z: 8 (z_hi: 4, z_lo: 2; z = z_hi * 2 + z_lo), core: 2. Of those that a mesh axis runs over, the one named last changes fastest.
Arguments:
- latents: bfloat16 [16, 3072, 3072], P('fsdp', ('uly', 'blk')), may hold values from -40 to 40
- sampler_noise: bfloat16 [16, 3072, 3072], P('fsdp', ('uly', 'blk')), may hold values from -6 to 6
- query_key_value_weight: bfloat16 [3, 3072, 1536], P(None, 'fsdp', 'uly'), may hold values from -0.375 to 0.375
- output_weight: bfloat16 [3072, 1536], P('fsdp', 'uly'), may hold values from -0.15625 to 0.15625
- adapter_down_map: bfloat16 [64, 1536], P(None, 'uly'), may hold values from -0.15625 to 0.15625
- adapter_up_map: bfloat16 [64, 3072], replicated, may hold values from -0.75 to 0.75
- valid_token_count: int32 [16], P('fsdp'), may hold values from 1536 to 3072
- advantage: float32 [16], P('fsdp'), may hold values from -3 to 3
- timestep_index: int32 [1], replicated, may hold values from 1 to 15
Outputs:
- next_latents: bfloat16 [16, 3072, 3072], P('fsdp', ('uly', 'blk'))
- log_ratio: float32 [16], P('fsdp')
- grad_down: float32 [64, 1536], P(None, 'uly')
- grad_up: float32 [64, 3072], replicated
All inputs are finite; a program needn't handle non-finite values.
Results may differ from a plain program's by a relative error of at most 0.0055.
The roundings to bfloat16 on the way count: a program that leaves them out, or rounds other values in their place, can miss the bound.
Values may be sent and summed in bfloat16 or wider, within the bound.
No kernel may reach another device: no remote copies, remote signals or barrier semaphores. Data moves between devices by JAX's collectives and lax.ppermute only.
A program may use at most 128 MiB of HBM per device.

v0:
```python
import math
import jax
import jax.numpy as jnp
from jax import lax
from jax.sharding import PartitionSpec as P

HEAD_SIZE = 128
STEPS = 16
noise_level = 0.7
loss_scale = 4194304.0
rms_eps = 1e-06


def shards(
    latents,
    sampler_noise,
    query_key_value_weight,
    output_weight,
    adapter_down_map,
    adapter_up_map,
    valid_token_count,
    advantage,
    timestep_index,
):
    current = latents[0].astype(jnp.float32)
    rows = current.shape[0]
    width = current.shape[1]
    normed = (current * lax.rsqrt(jnp.mean(current * current, -1, keepdims=True) + rms_eps)).astype(
        jnp.bfloat16
    )
    gathered = lax.all_gather(normed, "uly", axis=0, tiled=True)
    projected = jnp.einsum(
        "td,kdh->kth",
        gathered,
        lax.all_gather(query_key_value_weight, "fsdp", axis=1, tiled=True),
        preferred_element_type=jnp.float32,
    ).astype(jnp.bfloat16)
    query_rows = projected[0]
    key_rows, value_rows = (
        lax.all_gather(projected[1], "blk", axis=0, tiled=True),
        lax.all_gather(projected[2], "blk", axis=0, tiled=True),
    )
    uly_count = lax.axis_size("uly")
    blk_count = lax.axis_size("blk")
    uly_id = lax.axis_index("uly")
    blk_id = lax.axis_index("blk")
    limit = valid_token_count[0]
    group_rows = uly_count * rows
    key_index = jnp.arange(key_rows.shape[0], dtype=jnp.int32)
    key_pos = (
        key_index % group_rows // rows * blk_count + key_index // group_rows
    ) * rows + key_index % rows
    key_ok = (key_pos < limit)[None, None, :]
    heads_here = query_rows.shape[1] // HEAD_SIZE
    query_split = query_rows.reshape(query_rows.shape[0], heads_here, HEAD_SIZE)
    key_split = key_rows.reshape(key_rows.shape[0], heads_here, HEAD_SIZE)
    value_split = value_rows.reshape(value_rows.shape[0], heads_here, HEAD_SIZE)
    scores = jnp.einsum(
        "qhd,khd->hqk", query_split, key_split, preferred_element_type=jnp.float32
    ) * (1.0 / math.sqrt(HEAD_SIZE))
    masked = jnp.where(key_ok, scores, -1e30)
    row_max = jnp.max(masked, -1, keepdims=True)
    exp_terms = jnp.where(key_ok, jnp.exp(masked - row_max), 0.0)
    weights = (exp_terms / jnp.sum(exp_terms, -1, keepdims=True)).astype(jnp.bfloat16)
    attention_output = jnp.einsum(
        "hqk,khd->qhd", weights, value_split, preferred_element_type=jnp.float32
    )
    attention_output = attention_output.astype(jnp.bfloat16).reshape(
        query_rows.shape[0], heads_here * HEAD_SIZE
    )
    weight_cols = lax.all_gather(output_weight, "fsdp", axis=0, tiled=True)
    contract_product = (((1,), (1,)), ((), ()))
    own_heads = lax.all_to_all(attention_output, "uly", split_axis=0, concat_axis=1, tiled=True)
    weight_full, down_full = (
        lax.all_gather(weight_cols, "uly", axis=1, tiled=True),
        lax.all_gather(adapter_down_map, "uly", axis=1, tiled=True),
    )
    velocity = lax.dot_general(
        own_heads, weight_full, contract_product, preferred_element_type=jnp.float32
    )
    narrow_projection = lax.dot_general(
        own_heads, down_full, contract_product, preferred_element_type=jnp.float32
    ).astype(jnp.bfloat16)
    adapter_result = jnp.dot(narrow_projection, adapter_up_map, preferred_element_type=jnp.float32)
    step_float = timestep_index[0].astype(jnp.float32)
    time_now = 1.0 - step_float / STEPS
    step_size = 1.0 / STEPS
    noise_std = noise_level * jnp.sqrt(time_now / (1.0 - time_now))
    drift_gain = 1.0 + noise_level**2 / 2.0
    ratio_gain = jnp.sqrt(step_size) * drift_gain / noise_std
    noise_f = sampler_noise[0].astype(jnp.float32)
    moved = current - step_size * (
        drift_gain * velocity + noise_level**2 * current / (2.0 * (1.0 - time_now))
    )
    next_latents = (moved + noise_std * jnp.sqrt(step_size) * noise_f).astype(jnp.bfloat16)[None]
    standard = noise_f + ratio_gain * adapter_result
    tok_pos = (uly_id * blk_count + blk_id) * rows + jnp.arange(rows, dtype=jnp.int32)
    tok_ok = (tok_pos < limit)[:, None]
    valid_len = limit.astype(jnp.float32)
    partial_log = jnp.sum(jnp.where(tok_ok, noise_f * noise_f - standard * standard, 0.0)) / (
        2.0 * valid_len * width
    )
    log_ratio = lax.psum(partial_log, ("uly", "blk"))
    coef = (
        loss_scale
        * advantage[0]
        * jnp.exp(log_ratio)
        * ratio_gain
        / (lax.axis_size("fsdp") * valid_len * width)
    )
    delta_gradient = (jnp.where(tok_ok, standard, 0.0) * coef).astype(jnp.bfloat16)
    first_axis = (((0,), (0,)), ((), ()))
    up_part = lax.dot_general(
        narrow_projection, delta_gradient, first_axis, preferred_element_type=jnp.float32
    )
    narrow_gradient = lax.dot_general(
        delta_gradient, adapter_up_map, contract_product, preferred_element_type=jnp.float32
    ).astype(jnp.bfloat16)
    down_part = lax.dot_general(
        narrow_gradient, own_heads, first_axis, preferred_element_type=jnp.float32
    )
    grad_up, down_total = lax.psum((up_part, down_part), ("fsdp", "uly", "blk"))
    local_columns = adapter_down_map.shape[1]
    grad_down = lax.dynamic_slice_in_dim(down_total, uly_id * local_columns, local_columns, 1)
    return (next_latents, jnp.reshape(log_ratio, (1,)), grad_down, grad_up)


def solution(mesh):
    placed = (
        P("fsdp", ("uly", "blk"), None),
        P("fsdp", ("uly", "blk"), None),
        P(None, "fsdp", "uly"),
        P("fsdp", "uly"),
        P(None, "uly"),
        P(),
        P("fsdp"),
        P("fsdp"),
        P(),
    )
    return jax.shard_map(
        shards,
        mesh=mesh,
        in_specs=placed,
        out_specs=(P("fsdp", ("uly", "blk"), None), P("fsdp"), P(None, "uly"), P()),
        check_vma=False,
    )
```

profile of v0, /device:TPU:1, one launch (start us, length us, event | category | flops | bytes accessed | tf_op | source)
XLA Modules:
  0.0 696.5 jit_solution(7782017306988435983)
XLA Ops:
  7.2 0.0 copy-start
  7.2 0.0 all-gather.9.cloned.1.call-start
  7.2 1.6 fusion.19
  8.9 2.6 fusion.20
  11.5 0.0 all-gather.9.cloned.1.call-update
  11.5 0.0 all-gather.11.cloned.1.call-start
  11.5 0.7 all-gather.11.cloned.1.call-update
  12.2 0.0 all-gather.19.cloned.1.call-start
  12.3 58.1 %all-gather.9.cloned.1.call-done = bf16[768,3072]{1,0:T(8,128)(2,1)} async-done(((bf16[192,3072]{1,0:T(8,128)(2,1)}), bf16[768,3072]{1,0:T(8,128)(2,1)}) %all-gather.9.cloned.1.call-update) | async-done | bytes 4718608 | tf_op jit(solution)/shard_map/all_gather | solution.py:31
  70.3 51.3 %all-gather.11.cloned.1.call-done = bf16[3,3072,384]{2,1,0:T(8,128)(2,1)} async-done(((bf16[3,192,384]{2,1,0:T(8,128)(2,1)}), bf16[3,3072,384]{2,1,0:T(8,128)(2,1)}) %all-gather.11.cloned.1.call-update) | async-done | bytes 7077904 | tf_op jit(solution)/shard_map/all_gather | solution.py:35
  121.7 10.3 %convert_bitcast_fusion = bf16[3,768,384]{1,2,0:T(8,128)(2,1)S(1)} fusion(bf16[3,3072,384]{2,1,0:T(8,128)(2,1)} %all-gather.11.cloned.1.call-done, bf16[768,3072]{1,0:T(8,128)(2,1)} %all-gather.9.cloned.1.call-done), kind=kOutput, calls=%fused_computation.33 | convolution fusion | flops 5436702720 | bytes 13565952 | tf_op jit(solution)/shard_map/td,kdh->kth/dot_general | solution.py:32
  132.0 1.1 fusion.53
  133.1 0.0 all-gather.19.cloned.1.call-update
  133.1 0.0 all-gather.17.cloned.1.call-start
  133.2 0.5 all-gather.17.cloned.1.call-update
  133.7 0.2 all-gather.13.cloned.1.call-start
  133.9 0.4 all-gather.13.cloned.1.call-update
  135.0 50.7 %all-gather.19.cloned.1.call-done = bf16[1,3072,384]{1,2,0:T(8,128)(2,1)} async-done(((bf16[1,768,384]{1,2,0:T(8,128)(2,1)}), bf16[1,3072,384]{1,2,0:T(8,128)(2,1)}) %all-gather.19.cloned.1.call-update) | async-done | bytes 2359312 | tf_op jit(solution)/shard_map/all_gather | solution.py:40
  185.6 16.2 %fusion.54 = (f32[3,768]{1,0:T(4,128)S(1)}, f32[3,768,3072]{2,1,0:T(8,128)}) fusion(pred[3072]{0:T(1024)(128)(4,1)S(1)} %fusion.47, bf16[768,3,128]{0,2,1:T(8,128)(2,1)S(1)} %bitcast.55, bf16[3072,3,128]{0,2,1:T(8,128)(2,1)} %bitcast.56), kind=kOutput, calls=%fused_computation.75 | convolution fusion | flops 1847331840 | bytes 31272960 | tf_op jit(solution)/shard_map/sub | solution.py:63
  201.9 44.3 %all-gather.17.cloned.1.call-done = bf16[1,3072,384]{1,2,0:T(8,128)(2,1)} async-done(((bf16[1,768,384]{1,2,0:T(8,128)(2,1)}), bf16[1,3072,384]{1,2,0:T(8,128)(2,1)}) %all-gather.17.cloned.1.call-update) | async-done | bytes 2359312 | tf_op jit(solution)/shard_map/all_gather | solution.py:41
  246.2 12.1 %fusion.25 = bf16[768,3,128]{0,2,1:T(8,128)(2,1)S(1)} fusion(bf16[3072,3,128]{0,2,1:T(8,128)(2,1)} %bitcast.57, f32[3,768,3072]{2,1,0:T(8,128)} %get-tuple-element.10, f32[3,768]{1,0:T(4,128)S(1)} %get-tuple-element.9), kind=kOutput, calls=%fused_computation.35 | convolution fusion | flops 1826390016 | bytes 31269888 | tf_op jit(solution)/shard_map/hqk,khd->qhd/dot_general | solution.py:65
  258.2 0.0 copy-start.3
  258.2 0.7 reshape.95
  258.9 1.4 copy.21
  260.3 3.5 all-to-all-start
  263.8 0.0 all-reduce.3.cloned.1.call-start
  265.3 0.0 copy-done.3
  265.3 12.0 %all_gather.27 = bf16[64,1536]{1,0:T(8,128)(2,1)S(1)} all-gather(bf16[64,384]{1,0:T(8,128)(2,1)S(1)} %copy-done.3), channel_id=1, replica_groups=mesh['fsdp'=16,'uly'=4,'blk'=4] {'uly'}, dimensions={1}, use_global_device_ids=true | all-gather | bytes 245760 | tf_op jit(solution)/shard_map/all_gather | solution.py:76
  277.4 0.0 all-to-all-done
  277.4 0.1 copy.22
  277.5 0.3 convolution_convert_fusion.1
  277.8 0.0 copy-done
  277.8 2.8 fusion.18
  281.2 36.3 %psum.21 = f32[]{:T(128)} all-reduce(f32[]{:T(128)S(6)} %div.64), channel_id=1, replica_groups=mesh['fsdp'=16,'uly'=4,'blk'=4] {'uly','blk'}, use_global_device_ids=true, to_apply=%region_4.5 | all-reduce | flops 1 | bytes 8 | tf_op jit(solution)/shard_map/psum | solution.py:103
  318.3 1.3 fusion.52
  319.6 1.7 fusion.26
  321.3 0.0 copy-start.1
  321.3 0.0 all-reduce.3.cloned.1.call-update
  321.3 0.0 all-gather.15.cloned.1.call-start
  321.4 0.0 all-gather.13.cloned.1.call-done
  321.4 0.7 all-gather.15.cloned.1.call-update
  322.1 262.3 %all-reduce.3.cloned.1.call-done = (f32[64,1536]{1,0:T(8,128)}, f32[64,3072]{1,0:T(8,128)}) async-done(((f32[64,1536]{1,0:T(8,128)}, f32[64,3072]{1,0:T(8,128)}), (f32[64,1536]{1,0:T(8,128)}, f32[64,3072]{1,0:T(8,128)})) %all-reduce.3.cloned.1.call-update) | async-done | bytes 1179664 | tf_op jit(solution)/shard_map/psum | solution.py:122
  584.4 1.5 constant_dynamic-slice_fusion
  586.0 0.0 copy-start.2
  586.0 94.5 %all-gather.15.cloned.1.call-done = bf16[3072,1536]{1,0:T(8,128)(2,1)} async-done(((bf16[3072,384]{1,0:T(8,128)(2,1)}), bf16[3072,1536]{1,0:T(8,128)(2,1)}) %all-gather.15.cloned.1.call-update) | async-done | bytes 9437200 | tf_op jit(solution)/shard_map/all_gather | solution.py:75
  680.5 0.0 copy-done.1
  680.5 8.3 %fusion.13 = bf16[1,192,3072]{2,1,0:T(8,128)(2,1)} fusion(bf16[192,1536]{1,0:T(8,128)(2,1)S(1)} %bitcast.53, bf16[3072,1536]{1,0:T(8,128)(2,1)} %all-gather.15.cloned.1.call-done, bf16[1,192,3072]{2,1,0:T(8,128)(2,1)} %param.10, bf16[1,192,3072]{2,1,0:T(8,128)(2,1)S(1)} %copy-done.1, f32[]{:T(128)S(6)} %mul.121, f32[]{:T(128)S(6)} %mul.118), kind=kOutput, calls=%fused_computation.22 | convolution fusion | flops 1818427392 | bytes 13565960 | tf_op jit(solution)/shard_map/dot_general | solution.py:78
  688.8 0.0 copy-done.2
  688.8 0.9 copy.28
  (3 shorter events, 0.0 us)
Async XLA Ops:
  7.2 270.6 %copy-start = (bf16[64,3072]{1,0:T(8,128)(2,1)S(1)}, bf16[64,3072]{1,0:T(8,128)(2,1)}, u32[]{:S(2)}) copy-start(bf16[64,3072]{1,0:T(8,128)(2,1)} %param.14) | copy-start | bytes 1179652
  7.2 63.2 %all-gather.9.cloned.1.call-start = ((), (), s32[]{:S(2)}) async-start(), calls=%async_computation.1 | async-start | bytes 5898240 | tf_op jit(solution)/shard_map/all_gather | solution.py:31
  11.5 110.2 %all-gather.11.cloned.1.call-start = ((), (), s32[]{:S(2)}) async-start(), calls=%async_computation.2 | async-start | bytes 7520256 | tf_op jit(solution)/shard_map/all_gather | solution.py:35
  12.2 173.4 %all-gather.19.cloned.1.call-start = ((), (), s32[]{:S(2)}) async-start(), calls=%async_computation.6 | async-start | bytes 2949120 | tf_op jit(solution)/shard_map/all_gather | solution.py:40
  133.1 113.0 %all-gather.17.cloned.1.call-start = ((), (), s32[]{:S(2)}) async-start(), calls=%async_computation.5 | async-start | bytes 2949120 | tf_op jit(solution)/shard_map/all_gather | solution.py:41
  133.7 187.7 %all-gather.13.cloned.1.call-start = ((), (), s32[]{:S(2)}) async-start(), calls=%async_computation.3 | async-start | bytes 2506752 | tf_op jit(solution)/shard_map/all_gather | solution.py:71
  258.2 7.1 %copy-start.3 = (bf16[64,384]{1,0:T(8,128)(2,1)S(1)}, bf16[64,384]{1,0:T(8,128)(2,1)}, u32[]{:S(2)}) copy-start(bf16[64,384]{1,0:T(8,128)(2,1)} %param.13) | copy-start | bytes 147460
  260.3 17.0 %all-to-all-start = ((bf16[4,192,384]{2,1,0:T(8,128)(2,1)}), bf16[4,192,384]{2,1,0:T(8,128)(2,1)S(1)}, u32[]{:S(2)}, u32[]{:S(2)}) async-start(bf16[4,192,384]{2,1,0:T(8,128)(2,1)} %copy.21), calls=%async_computation | async-start | bytes 1179648 | tf_op jit(solution)/shard_map/all_to_all | solution.py:73
  263.8 320.6 %all-reduce.3.cloned.1.call-start = ((), (), s32[]{:S(2)}) async-start(), calls=%async_computation.7 | async-start | bytes 2359296 | tf_op jit(solution)/shard_map/psum | solution.py:122
  321.3 359.2 %copy-start.1 = (bf16[1,192,3072]{2,1,0:T(8,128)(2,1)S(1)}, bf16[1,192,3072]{2,1,0:T(8,128)(2,1)}, u32[]{:S(2)}) copy-start(bf16[1,192,3072]{2,1,0:T(8,128)(2,1)} %param.9) | copy-start | bytes 3538948
  321.3 359.2 %all-gather.15.cloned.1.call-start = ((), (), s32[]{:S(2)}) async-start(), calls=%async_computation.4 | async-start | bytes 11796480 | tf_op jit(solution)/shard_map/all_gather | solution.py:75
  586.0 102.8 %copy-start.2 = (f32[64,3072]{1,0:T(8,128)S(1)}, f32[64,3072]{1,0:T(8,128)}, u32[]{:S(2)}) copy-start(f32[64,3072]{1,0:T(8,128)} %get-tuple-element.16) | copy-start | bytes 2359300
Sparse Core Ops, SparseCore 0:
  11.6 58.6 all-gather.8
  72.1 49.4 all-gather.10
  133.3 52.3 all-gather.18
  187.9 58.2 all-gather.16
  247.8 35.5 all-gather.12
  321.4 262.9 all-reduce.2
  586.3 94.2 all-gather.14
where the time goes:
time: 697 us
  waiting for transfers between devices  564 us (81%)
  matrix products  53 us (8%)
  blocking collectives  48.4 us (7%)
  between operations  17.7 us (3%)
    psum x1, waiting for transfers between devices, shards(): grad_up, down_total = lax.psum((up_part, down_part), ('fsdp', 'uly', 'blk'))  262 us
    all_gather x1, waiting for transfers between devices, shards(): lax.all_gather(weight_cols, 'uly', axis=1, tiled=True)  94.5 us
    all_gather x1, waiting for transfers between devices, shards(): gathered = lax.all_gather(normed, 'uly', axis=0, tiled=True)  58.1 us
    all_gather x1, waiting for transfers between devices, shards(): lax.all_gather(query_key_value_weight, 'fsdp', axis=1, tiled=True)  51.3 us
    all_gather x1, waiting for transfers between devices, shards(): lax.all_gather(projected[1], 'blk', axis=0, tiled=True)  50.7 us
    all_gather x1, waiting for transfers between devices, shards(): lax.all_gather(projected[2], 'blk', axis=0, tiled=True)  44.3 us
    psum x1, blocking collectives, shards(): log_ratio = lax.psum(partial_log, ('uly', 'blk'))  36.3 us
    sub x1, matrix products, shards(): exp_terms = jnp.where(key_ok, jnp.exp(masked - row_max), 0.0)  16.2 us
  transfers between devices with their start and end apart: 8, of which 6 were waited for; matrix products, arithmetic and copies ran while one was open for 5% of the time, Pallas kernels for 0%

commit v1 on v0

--- a/solution.py
+++ b/solution.py
@@ -119,7 +119,7 @@
     down_part = lax.dot_general(
         narrow_gradient, own_heads, first_axis, preferred_element_type=jnp.float32
     )
-    grad_up, down_total = lax.psum((up_part, down_part), ("fsdp", "uly", "blk"))
+    grad_up, down_total = lax.psum(lax.psum((up_part, down_part), "fsdp"), ("uly", "blk"))
     local_columns = adapter_down_map.shape[1]
     grad_down = lax.dynamic_slice_in_dim(down_total, uly_id * local_columns, local_columns, 1)
     return (next_latents, jnp.reshape(log_ratio, (1,)), grad_down, grad_up)

time: 697 us -> 734 us (1.053); the launches traced: 697 us -> 724 us
  waiting for transfers between devices: 564 us -> 590 us
    psum x1 -> x2, waiting for transfers between devices: 262 us -> 286 us  [the longest x1 157 us: shards(): lax.psum(lax.psum((up_part, down_part), 'fsdp'), ('uly', 'blk'))]
  transfers between devices with their start and end apart: 8 -> 9, of which waited for: 6 -> 7; matrix products, arithmetic and copies ran while one was open for 5% -> 6% of each run, Pallas kernels for 0% -> 0%
where the time goes in v1:
time: 734 us; the launch traced here: 724 us
  waiting for transfers between devices  590 us (80%)
  matrix products  52.7 us (7%)
  blocking collectives  48.4 us (7%)
  between operations  17.7 us (2%)
    psum x1, waiting for transfers between devices, shards(): lax.psum(lax.psum((up_part, down_part), 'fsdp'), ('uly', 'blk'))  157 us
    psum x1, waiting for transfers between devices, shards(): lax.psum((up_part, down_part), 'fsdp')  129 us
    all_gather x1, waiting for transfers between devices, shards(): lax.all_gather(weight_cols, 'uly', axis=1, tiled=True)  96.7 us
    all_gather x1, waiting for transfers between devices, shards(): gathered = lax.all_gather(normed, 'uly', axis=0, tiled=True)  58.1 us
    all_gather x1, waiting for transfers between devices, shards(): lax.all_gather(query_key_value_weight, 'fsdp', axis=1, tiled=True)  51.3 us
    all_gather x1, waiting for transfers between devices, shards(): lax.all_gather(projected[1], 'blk', axis=0, tiled=True)  50.7 us
    all_gather x1, waiting for transfers between devices, shards(): lax.all_gather(projected[2], 'blk', axis=0, tiled=True)  44.3 us
    psum x1, blocking collectives, shards(): log_ratio = lax.psum(partial_log, ('uly', 'blk'))  36.3 us
  transfers between devices with their start and end apart: 9, of which 7 were waited for; matrix products, arithmetic and copies ran while one was open for 6% of the time, Pallas kernels for 0%

profile of v1, /device:TPU:1, one launch (start us, length us, event | category | flops | bytes accessed | tf_op | source)
XLA Modules:
  0.0 723.5 jit_solution(6406949666638955393)
XLA Ops:
  7.2 0.0 copy-start
  7.2 0.0 all-gather.9.cloned.1.call-start
  7.2 1.6 fusion.19
  8.9 2.6 fusion.20
  11.5 0.0 all-gather.9.cloned.1.call-update
  11.5 0.0 all-gather.11.cloned.1.call-start
  11.5 0.7 all-gather.11.cloned.1.call-update
  12.2 0.0 all-gather.19.cloned.1.call-start
  12.3 58.1 %all-gather.9.cloned.1.call-done = bf16[768,3072]{1,0:T(8,128)(2,1)} async-done(((bf16[192,3072]{1,0:T(8,128)(2,1)}), bf16[768,3072]{1,0:T(8,128)(2,1)}) %all-gather.9.cloned.1.call-update) | async-done | bytes 4718608 | tf_op jit(solution)/shard_map/all_gather | solution.py:31
  70.3 51.3 %all-gather.11.cloned.1.call-done = bf16[3,3072,384]{2,1,0:T(8,128)(2,1)} async-done(((bf16[3,192,384]{2,1,0:T(8,128)(2,1)}), bf16[3,3072,384]{2,1,0:T(8,128)(2,1)}) %all-gather.11.cloned.1.call-update) | async-done | bytes 7077904 | tf_op jit(solution)/shard_map/all_gather | solution.py:35
  121.7 10.3 %convert_bitcast_fusion = bf16[3,768,384]{1,2,0:T(8,128)(2,1)S(1)} fusion(bf16[3,3072,384]{2,1,0:T(8,128)(2,1)} %all-gather.11.cloned.1.call-done, bf16[768,3072]{1,0:T(8,128)(2,1)} %all-gather.9.cloned.1.call-done), kind=kOutput, calls=%fused_computation.33 | convolution fusion | flops 5436702720 | bytes 13565952 | tf_op jit(solution)/shard_map/td,kdh->kth/dot_general | solution.py:32
  132.0 1.1 fusion.53
  133.1 0.0 all-gather.19.cloned.1.call-update
  133.1 0.0 all-gather.17.cloned.1.call-start
  133.2 0.5 all-gather.17.cloned.1.call-update
  133.7 0.2 all-gather.13.cloned.1.call-start
  133.9 0.4 all-gather.13.cloned.1.call-update
  135.0 50.7 %all-gather.19.cloned.1.call-done = bf16[1,3072,384]{1,2,0:T(8,128)(2,1)} async-done(((bf16[1,768,384]{1,2,0:T(8,128)(2,1)}), bf16[1,3072,384]{1,2,0:T(8,128)(2,1)}) %all-gather.19.cloned.1.call-update) | async-done | bytes 2359312 | tf_op jit(solution)/shard_map/all_gather | solution.py:40
  185.6 16.2 %fusion.54 = (f32[3,768]{1,0:T(4,128)S(1)}, f32[3,768,3072]{2,1,0:T(8,128)}) fusion(pred[3072]{0:T(1024)(128)(4,1)S(1)} %fusion.47, bf16[768,3,128]{0,2,1:T(8,128)(2,1)S(1)} %bitcast.55, bf16[3072,3,128]{0,2,1:T(8,128)(2,1)} %bitcast.56), kind=kOutput, calls=%fused_computation.75 | convolution fusion | flops 1847331840 | bytes 31272960 | tf_op jit(solution)/shard_map/sub | solution.py:63
  201.9 44.3 %all-gather.17.cloned.1.call-done = bf16[1,3072,384]{1,2,0:T(8,128)(2,1)} async-done(((bf16[1,768,384]{1,2,0:T(8,128)(2,1)}), bf16[1,3072,384]{1,2,0:T(8,128)(2,1)}) %all-gather.17.cloned.1.call-update) | async-done | bytes 2359312 | tf_op jit(solution)/shard_map/all_gather | solution.py:41
  246.2 12.1 %fusion.25 = bf16[768,3,128]{0,2,1:T(8,128)(2,1)S(1)} fusion(bf16[3072,3,128]{0,2,1:T(8,128)(2,1)} %bitcast.57, f32[3,768,3072]{2,1,0:T(8,128)} %get-tuple-element.12, f32[3,768]{1,0:T(4,128)S(1)} %get-tuple-element.11), kind=kOutput, calls=%fused_computation.35 | convolution fusion | flops 1826390016 | bytes 31269888 | tf_op jit(solution)/shard_map/hqk,khd->qhd/dot_general | solution.py:65
  258.2 0.0 copy-start.2
  258.2 0.7 reshape.95
  258.9 1.4 copy.21
  260.3 3.5 all-to-all-start
  263.8 0.0 all-reduce.7.cloned.1.call-start
  265.3 0.0 copy-done.2
  265.3 12.0 %all_gather.27 = bf16[64,1536]{1,0:T(8,128)(2,1)S(1)} all-gather(bf16[64,384]{1,0:T(8,128)(2,1)S(1)} %copy-done.2), channel_id=1, replica_groups=mesh['fsdp'=16,'uly'=4,'blk'=4] {'uly'}, dimensions={1}, use_global_device_ids=true | all-gather | bytes 245760 | tf_op jit(solution)/shard_map/all_gather | solution.py:76
  277.4 0.0 all-to-all-done
  277.4 0.1 copy.22
  277.5 0.3 convolution_convert_fusion.1
  277.8 0.0 copy-done
  277.8 2.8 fusion.18
  281.2 36.3 %psum.35 = f32[]{:T(128)} all-reduce(f32[]{:T(128)S(6)} %div.64), channel_id=1, replica_groups=mesh['fsdp'=16,'uly'=4,'blk'=4] {'uly','blk'}, use_global_device_ids=true, to_apply=%region_4.5 | all-reduce | flops 1 | bytes 8 | tf_op jit(solution)/shard_map/psum | solution.py:103
  318.3 1.3 fusion.52
  319.6 1.7 fusion.26
  321.3 0.0 copy-start.1
  321.3 0.0 copy-start.3
  321.3 0.0 all-reduce.7.cloned.1.call-update
  321.3 0.0 all-gather.15.cloned.1.call-start
  321.4 0.0 all-gather.13.cloned.1.call-done
  321.4 0.7 all-gather.15.cloned.1.call-update
  322.1 0.0 all-reduce.5.cloned.1.call-start
  322.1 129.2 %all-reduce.7.cloned.1.call-done = (f32[64,1536]{1,0:T(8,128)}, f32[64,3072]{1,0:T(8,128)}) async-done(((f32[64,1536]{1,0:T(8,128)}, f32[64,3072]{1,0:T(8,128)}), (f32[64,1536]{1,0:T(8,128)}, f32[64,3072]{1,0:T(8,128)})) %all-reduce.7.cloned.1.call-update) | async-done | bytes 1179664 | tf_op jit(solution)/shard_map/psum | solution.py:122
  451.4 0.0 all-reduce.5.cloned.1.call-update
  451.4 96.7 %all-gather.15.cloned.1.call-done = bf16[3072,1536]{1,0:T(8,128)(2,1)} async-done(((bf16[3072,384]{1,0:T(8,128)(2,1)}), bf16[3072,1536]{1,0:T(8,128)(2,1)}) %all-gather.15.cloned.1.call-update) | async-done | bytes 9437200 | tf_op jit(solution)/shard_map/all_gather | solution.py:75
  548.1 0.0 copy-done.1
  548.1 0.0 copy-done.3
  548.1 8.0 %fusion.13 = bf16[1,192,3072]{2,1,0:T(8,128)(2,1)} fusion(bf16[192,1536]{1,0:T(8,128)(2,1)S(1)} %bitcast.53, bf16[3072,1536]{1,0:T(8,128)(2,1)} %all-gather.15.cloned.1.call-done, bf16[1,192,3072]{2,1,0:T(8,128)(2,1)S(1)} %copy-done.3, bf16[1,192,3072]{2,1,0:T(8,128)(2,1)S(1)} %copy-done.1, f32[]{:T(128)S(6)} %mul.121, f32[]{:T(128)S(6)} %mul.118), kind=kOutput, calls=%fused_computation.22 | convolution fusion | flops 1818427392 | bytes 13565960 | tf_op jit(solution)/shard_map/dot_general | solution.py:78
  556.1 157.0 %all-reduce.5.cloned.1.call-done = (f32[64,1536]{1,0:T(8,128)}, f32[64,3072]{1,0:T(8,128)}) async-done(((f32[64,1536]{1,0:T(8,128)}, f32[64,3072]{1,0:T(8,128)}), (f32[64,1536]{1,0:T(8,128)}, f32[64,3072]{1,0:T(8,128)})) %all-reduce.5.cloned.1.call-update) | async-done | bytes 1179664 | tf_op jit(solution)/shard_map/psum | solution.py:122
  713.1 1.5 constant_dynamic-slice_fusion
  714.6 2.1 copy.30
  (3 shorter events, 0.0 us)
Async XLA Ops:
  7.2 270.6 %copy-start = (bf16[64,3072]{1,0:T(8,128)(2,1)S(1)}, bf16[64,3072]{1,0:T(8,128)(2,1)}, u32[]{:S(2)}) copy-start(bf16[64,3072]{1,0:T(8,128)(2,1)} %param.14) | copy-start | bytes 1179652
  7.2 63.2 %all-gather.9.cloned.1.call-start = ((), (), s32[]{:S(2)}) async-start(), calls=%async_computation.1 | async-start | bytes 5898240 | tf_op jit(solution)/shard_map/all_gather | solution.py:31
  11.5 110.2 %all-gather.11.cloned.1.call-start = ((), (), s32[]{:S(2)}) async-start(), calls=%async_computation.2 | async-start | bytes 7520256 | tf_op jit(solution)/shard_map/all_gather | solution.py:35
  12.2 173.4 %all-gather.19.cloned.1.call-start = ((), (), s32[]{:S(2)}) async-start(), calls=%async_computation.6 | async-start | bytes 2949120 | tf_op jit(solution)/shard_map/all_gather | solution.py:40
  133.1 113.0 %all-gather.17.cloned.1.call-start = ((), (), s32[]{:S(2)}) async-start(), calls=%async_computation.5 | async-start | bytes 2949120 | tf_op jit(solution)/shard_map/all_gather | solution.py:41
  133.7 187.7 %all-gather.13.cloned.1.call-start = ((), (), s32[]{:S(2)}) async-start(), calls=%async_computation.3 | async-start | bytes 2506752 | tf_op jit(solution)/shard_map/all_gather | solution.py:71
  258.2 7.1 copy-start.2
  260.3 17.0 %all-to-all-start = ((bf16[4,192,384]{2,1,0:T(8,128)(2,1)}), bf16[4,192,384]{2,1,0:T(8,128)(2,1)S(1)}, u32[]{:S(2)}, u32[]{:S(2)}) async-start(bf16[4,192,384]{2,1,0:T(8,128)(2,1)} %copy.21), calls=%async_computation | async-start | bytes 1179648 | tf_op jit(solution)/shard_map/all_to_all | solution.py:73
  263.8 187.5 %all-reduce.7.cloned.1.call-start = ((), (), s32[]{:S(2)}) async-start(), calls=%async_computation.8 | async-start | bytes 2359296 | tf_op jit(solution)/shard_map/psum | solution.py:122
  321.3 226.8 %copy-start.1 = (bf16[1,192,3072]{2,1,0:T(8,128)(2,1)S(1)}, bf16[1,192,3072]{2,1,0:T(8,128)(2,1)}, u32[]{:S(2)}) copy-start(bf16[1,192,3072]{2,1,0:T(8,128)(2,1)} %param.9) | copy-start | bytes 3538948
  321.3 226.8 %copy-start.3 = (bf16[1,192,3072]{2,1,0:T(8,128)(2,1)S(1)}, bf16[1,192,3072]{2,1,0:T(8,128)(2,1)}, u32[]{:S(2)}) copy-start(bf16[1,192,3072]{2,1,0:T(8,128)(2,1)} %param.10) | copy-start | bytes 3538948
  321.3 226.7 %all-gather.15.cloned.1.call-start = ((), (), s32[]{:S(2)}) async-start(), calls=%async_computation.4 | async-start | bytes 11796480 | tf_op jit(solution)/shard_map/all_gather | solution.py:75
  322.1 391.0 %all-reduce.5.cloned.1.call-start = ((), (), s32[]{:S(2)}) async-start(), calls=%async_computation.7 | async-start | bytes 2359296 | tf_op jit(solution)/shard_map/psum | solution.py:122
Sparse Core Ops, SparseCore 0:
  11.6 58.6 all-gather.8
  72.1 49.4 all-gather.10
  133.3 52.3 all-gather.18
  187.9 58.2 all-gather.16
  247.8 35.5 all-gather.12
  321.4 129.8 all-reduce.6
  453.2 94.8 all-gather.14
  550.8 162.2 all-reduce.4
